TPU v7x, 256 devices: a whole 4x4x8 slice. The times are simulated.
256 devices in a mesh: wide: 32 (over y, z), narrow: 8 (over x, core).
Axes of the slice: x: 4, y: 4, z: 8, core: 2. Of those that a mesh axis runs over, the one named last changes fastest.
Arguments:
- activations: bfloat16 [1024, 28672], P('wide', 'narrow'), may hold values from -6 to 6
- out_grads: bfloat16 [1024, 8192], P('wide'), may hold values from -6 to 6
- basis_in: bfloat16 [28672, 28672], P('narrow', 'wide'), may hold values from -0.03125 to 0.03125
- basis_out: bfloat16 [8192, 8192], P('wide', 'narrow'), may hold values from -0.0625 to 0.0625
- eigenvalues: bfloat16 [8192, 28672], P('narrow', 'wide'), may hold values from 0.29882812 to 10
- queries: bfloat16 [2, 8192, 28672], P(None, 'narrow', 'wide'), may hold values from -0.00036621094 to 0.00036621094
- doc_ids: int32 [1024], replicated, may hold values from 0 to 63, never falling along the last dimension, each value on 1 to 32 neighbouring positions
Outputs:
- scores: float32 [64, 2], replicated
Inputs may be any that keep to these rules, and one draw needn't show every extreme that they name: `doc_ids`: document numbers never fall along the tokens; each document has 1 to 32 tokens.
All inputs are finite; a program needn't handle non-finite values.
Results may differ from a plain program's by a relative error of at most 0.0051.
Values may be sent and summed in bfloat16 or wider, within the bound.
No kernel may reach another device: no remote copies, remote signals or barrier semaphores. Data moves between devices by JAX's collectives and lax.ppermute only.
A program may use at most 128 MiB of HBM per device.

v0:
```python
import functools
import jax
import jax.numpy as jnp
from jax import lax
from jax.sharding import Mesh
from jax.sharding import PartitionSpec as P

DOC_PER = 2
WIDE = ("wide_0", "wide_1")
NARROW = ("narrow_0", "narrow_1")
WIDE_NARROW = ("wide_0", "wide_1", "narrow_0", "narrow_1")
DAMPING = 0.1


def over_axes(value, axes):
    return functools.reduce(lax.psum, axes, value)


def shards(activations, out_grads, basis_in, basis_out, eigenvalues, queries, doc_ids):
    partial_acts = jnp.dot(
        lax.all_gather(activations, WIDE, axis=0, tiled=True),
        basis_in,
        preferred_element_type=jnp.float32,
    )
    rot_acts = lax.psum(partial_acts, NARROW).astype(jnp.bfloat16)
    rows_held = lax.all_to_all(out_grads, WIDE, split_axis=1, concat_axis=0, tiled=True)
    partial_grads = jnp.dot(rows_held, basis_out, preferred_element_type=jnp.float32)
    rot_grads = lax.psum(partial_grads, WIDE).astype(jnp.bfloat16)
    precond = (
        queries.astype(jnp.float32) / (eigenvalues.astype(jnp.float32)[None] + DAMPING)
    ).astype(jnp.bfloat16)
    mixed_rows = jnp.einsum("ti,qij->qtj", rot_grads, precond, preferred_element_type=jnp.float32)
    token_part = jnp.sum(mixed_rows * rot_acts.astype(jnp.float32)[None], axis=2)
    doc_count = DOC_PER * lax.axis_size(WIDE)
    member = (doc_ids[None, :] == jnp.arange(doc_count, dtype=jnp.int32)[:, None]).astype(
        jnp.float32
    )
    partial_docs = jnp.dot(member, token_part.T, precision=lax.Precision.HIGHEST)
    return over_axes(partial_docs, WIDE_NARROW)


def solution(mesh):
    finer = Mesh(mesh.devices.reshape(4, 8, 4, 2), ("wide_0", "wide_1", "narrow_0", "narrow_1"))
    in_specs = (
        P(WIDE, NARROW),
        P(WIDE, None),
        P(NARROW, WIDE),
        P(WIDE, NARROW),
        P(NARROW, WIDE),
        P(None, NARROW, WIDE),
        P(),
    )
    out_specs = P()
    return jax.shard_map(
        shards, mesh=finer, in_specs=in_specs, out_specs=out_specs, check_vma=False
    )
```

profile of v0, /device:TPU:1, one launch (start us, length us, event | category | flops | bytes accessed | tf_op | source)
XLA Modules:
  0.0 354.1 jit_solution(14083641496422181634)
XLA Ops:
  6.5 0.0 copy-start
  6.5 0.0 all-gather.2.cloned.1.call-start
  6.5 0.7 all-gather.2.cloned.1.call-update
  7.3 1.9 copy.17
  9.2 12.0 %all-to-all-start = ((bf16[32,32,256]{2,0,1:T(8,128)(2,1)}), bf16[32,32,256]{2,0,1:T(8,128)(2,1)S(1)}, u32[]{:S(2)}, u32[]{:S(2)}) async-start(bf16[32,32,256]{2,0,1:T(8,128)(2,1)} %bitcast.20), calls=%async_computation | async-start | bytes 1048576 | tf_op jit(solution)/shard_map/all_to_all | solution.py:26
  21.2 3.7 %convert_add_fusion = f32[1024,896]{1,0:T(8,128)} fusion(bf16[1024,896]{1,0:T(8,128)(2,1)} %param.11), kind=kLoop, calls=%fused_computation.5 | loop fusion | flops 1835008 | bytes 5505024 | tf_op jit(solution)/shard_map/add | solution.py:30
  24.9 10.8 %all-to-all-done = bf16[32,32,256]{2,0,1:T(8,128)(2,1)S(1)} async-done(((bf16[32,32,256]{2,0,1:T(8,128)(2,1)}), bf16[32,32,256]{2,0,1:T(8,128)(2,1)S(1)}, u32[]{:S(2)}, u32[]{:S(2)}) %all-to-all-start) | async-done | bytes 524320 | tf_op jit(solution)/shard_map/all_to_all | solution.py:26
  35.7 0.0 copy-done
  35.7 2.8 fusion.9
  38.5 172.0 %all-reduce.3 = bf16[1024,1024]{1,0:T(8,128)(2,1)} all-reduce(f32[1024,1024]{1,0:T(8,128)} %fusion.9), channel_id=1, replica_groups=mesh['wide_0'=4,'wide_1'=8,'narrow_0'=4,'narrow_1'=2] {'wide_0','wide_1'}, use_global_device_ids=true, to_apply=%region_0.0 | all-reduce | flops 1048576 | bytes 6291456 | tf_op jit(solution)/shard_map/psum | solution.py:28
  210.5 0.0 all-gather.2.cloned.1.call-done
  210.5 13.1 %fusion.10 = f32[1024,896]{1,0:T(8,128)} fusion(bf16[1024,3584]{1,0:T(8,128)(2,1)} %all-gather.2.cloned.1.call-done, bf16[3584,896]{1,0:T(8,128)(2,1)} %param.9), kind=kOutput, calls=%fused_computation.14 | convolution fusion | flops 6576668672 | bytes 17432576 | tf_op jit(solution)/shard_map/dot_general | solution.py:20
  223.6 77.3 %all-reduce.2 = bf16[1024,896]{1,0:T(8,128)(2,1)S(1)} all-reduce(f32[1024,896]{1,0:T(8,128)} %fusion.10), channel_id=1, replica_groups=mesh['wide_0'=4,'wide_1'=8,'narrow_0'=4,'narrow_1'=2] {'narrow_0','narro..., use_global_device_ids=true, to_apply=%region_1.0 | all-reduce | flops 917504 | bytes 5505024 | tf_op jit(solution)/shard_map/psum | solution.py:25
  300.9 2.9 copy.13
  303.8 0.0 copy-start.1
  303.8 8.9 %fusion = f32[2,1024]{1,0:T(2,128)S(1)} fusion(f32[1024,896]{0,1:T(8,128)} %copy.13, bf16[1024,1024]{1,0:T(8,128)(2,1)} %all-reduce.3, bf16[2,1024,896]{2,1,0:T(8,128)(2,1)} %param.12, f32[1024,896]{1,0:T(8,128)} %convert_add_fusion), kind=kOutput, calls=%fused_computation.1 | convolution fusion | flops 3767269376 | bytes 13115392 | tf_op jit(solution)/shard_map/ti,qij->qtj/dot_general | solution.py:32
  312.7 0.0 copy-done.1
  312.7 0.2 fusion.7
  312.9 6.0 %psum.44 = f32[64,2]{0,1:T(2,128)S(1)} all-reduce(f32[64,2]{0,1:T(2,128)S(1)} %fusion.7), channel_id=1, replica_groups=mesh['wide_0'=4,'wide_1'=8,'narrow_0'=4,'narrow_1'=2] {'wide_0'}, use_global_device_ids=true, to_apply=%region_3.0 | all-reduce | flops 128 | bytes 1024 | tf_op jit(solution)/shard_map/psum | solution.py:16
  319.0 10.7 %psum.45 = f32[64,2]{0,1:T(2,128)S(1)} all-reduce(f32[64,2]{0,1:T(2,128)S(1)} %psum.44), channel_id=1, replica_groups=mesh['wide_0'=4,'wide_1'=8,'narrow_0'=4,'narrow_1'=2] {'wide_1'}, use_global_device_ids=true, to_apply=%region_4.0 | all-reduce | flops 128 | bytes 1024 | tf_op jit(solution)/shard_map/psum | solution.py:16
  329.6 9.9 %psum.46 = f32[64,2]{0,1:T(2,128)S(1)} all-reduce(f32[64,2]{0,1:T(2,128)S(1)} %psum.45), channel_id=1, replica_groups=mesh['wide_0'=4,'wide_1'=8,'narrow_0'=4,'narrow_1'=2] {'narrow_0'}, use_global_device_ids=true, to_apply=%region_5.0 | all-reduce | flops 128 | bytes 1024 | tf_op jit(solution)/shard_map/psum | solution.py:16
  339.6 7.7 %psum.47 = f32[64,2]{0,1:T(2,128)} all-reduce(f32[64,2]{0,1:T(2,128)S(1)} %psum.46), channel_id=1, replica_groups=mesh['wide_0'=4,'wide_1'=8,'narrow_0'=4,'narrow_1'=2] {'narrow_1'}, use_global_device_ids=true, to_apply=%region_6.0 | all-reduce | flops 128 | bytes 1024 | tf_op jit(solution)/shard_map/psum | solution.py:16
Async XLA Ops:
  6.5 29.2 %copy-start = (bf16[256,1024]{1,0:T(8,128)(2,1)S(1)}, bf16[256,1024]{1,0:T(8,128)(2,1)}, u32[]{:S(2)}) copy-start(bf16[256,1024]{1,0:T(8,128)(2,1)} %param.10) | copy-start | bytes 1572868
  6.5 204.0 %all-gather.2.cloned.1.call-start = ((), (), s32[]{:S(2)}) async-start(), calls=%async_computation.1 | async-start | bytes 7569408 | tf_op jit(solution)/shard_map/all_gather | solution.py:21
  9.2 26.6 %all-to-all-start = ((bf16[32,32,256]{2,0,1:T(8,128)(2,1)}), bf16[32,32,256]{2,0,1:T(8,128)(2,1)S(1)}, u32[]{:S(2)}, u32[]{:S(2)}) async-start(bf16[32,32,256]{2,0,1:T(8,128)(2,1)} %bitcast.20), calls=%async_computation | async-start | bytes 1048576 | tf_op jit(solution)/shard_map/all_to_all | solution.py:26
  303.8 8.9 %copy-start.1 = (s32[1024]{0:T(1024)S(1)}, s32[1024]{0:T(1024)}, u32[]{:S(2)}) copy-start(s32[1024]{0:T(1024)} %param.13) | copy-start | bytes 12292
Sparse Core Ops, SparseCore 0:
  9.9 126.6 all-gather.1
where the time goes:
time: 354 us
  blocking collectives  284 us (80%)
  matrix products  25 us (7%)
  between operations  13.4 us (4%)
  starting transfers between devices  12 us (3%)
  waiting for transfers between devices  11.5 us (3%)
  local copies, waits for them, and re-layouts  4.81 us (1%)
  other arithmetic  3.7 us (1%)
    psum x1, blocking collectives, shards(): rot_grads = lax.psum(partial_grads, WIDE).astype(jnp.bfloat16)  172 us
    psum x1, blocking collectives, shards(): rot_acts = lax.psum(partial_acts, NARROW).astype(jnp.bfloat16)  77.3 us
    psum x4, blocking collectives, over_axes(): return functools.reduce(lax.psum, axes, value)  34.3 us
    dot_general x1, matrix products, shards(): jnp.dot(lax.all_gather(activations, WIDE, axis=0, tiled=True), basis_in,...  13.1 us
    all_to_all x1, starting transfers between devices, shards(): lax.all_to_all(out_grads, WIDE, split_axis=1, concat_axis=0, tiled=True)  12 us
    all_to_all x1, waiting for transfers between devices, shards(): lax.all_to_all(out_grads, WIDE, split_axis=1, concat_axis=0, tiled=True)  10.8 us
    dot_general x1, matrix products, shards(): jnp.einsum('ti,qij->qtj', rot_grads, precond, preferred_element_type=jnp....  8.92 us
  transfers between devices with their start and end apart: 2, of which 1 were waited for; matrix products, arithmetic and copies ran while one was open for 2% of the time, Pallas kernels for 0%

commit v1 on v0

--- a/solution.py
+++ b/solution.py
@@ -25,7 +25,7 @@
     rot_acts = lax.psum(partial_acts, NARROW).astype(jnp.bfloat16)
     rows_held = lax.all_to_all(out_grads, WIDE, split_axis=1, concat_axis=0, tiled=True)
     partial_grads = jnp.dot(rows_held, basis_out, preferred_element_type=jnp.float32)
-    rot_grads = lax.psum(partial_grads, WIDE).astype(jnp.bfloat16)
+    rot_grads = lax.psum(lax.psum(partial_grads, "wide_1"), "wide_0").astype(jnp.bfloat16)
     precond = (
         queries.astype(jnp.float32) / (eigenvalues.astype(jnp.float32)[None] + DAMPING)
     ).astype(jnp.bfloat16)

time: 354 us -> 390 us (1.10)
  waiting for transfers between devices: 11.5 us -> 147 us
  blocking collectives: 284 us -> 196 us
  starting transfers between devices: 12 us -> 0.05 us
    psum x0 -> x1, waiting for transfers between devices: none -> 147 us  [shards(): lax.psum(partial_grads, 'wide_1')]
    psum x1, blocking collectives: 172 us -> 77.2 us  [shards(): lax.psum(lax.psum(partial_grads, 'wide_1'), 'wide_0').astype(jnp.bfloat16)]
    all_to_all x0 -> x1, blocking collectives: none -> 26.1 us  [shards(): lax.all_to_all(out_grads, WIDE, split_axis=1, concat_axis=0, tiled=True)]
    psum x1, blocking collectives: 77.3 us -> 56.4 us  [shards(): rot_acts = lax.psum(partial_acts, NARROW).astype(jnp.bfloat16)]
    all_to_all x1 -> x0, starting transfers between devices: 12 us -> none  [shards(): lax.all_to_all(out_grads, WIDE, split_axis=1, concat_axis=0, tiled=True)]
    all_to_all x1 -> x0, waiting for transfers between devices: 10.8 us -> none  [shards(): lax.all_to_all(out_grads, WIDE, split_axis=1, concat_axis=0, tiled=True)]
  transfers between devices with their start and end apart: 2 -> 2, of which waited for: 1 -> 1; matrix products, arithmetic and copies ran while one was open for 2% -> 1% of each run, Pallas kernels for 0% -> 0%
where the time goes in v1:
time: 390 us
  blocking collectives  196 us (50%)
  waiting for transfers between devices  147 us (38%)
  matrix products  24.9 us (6%)
  between operations  14.9 us (4%)
  local copies, waits for them, and re-layouts  4.97 us (1%)
    psum x1, waiting for transfers between devices, shards(): lax.psum(partial_grads, 'wide_1')  147 us
    psum x1, blocking collectives, shards(): lax.psum(lax.psum(partial_grads, 'wide_1'), 'wide_0').astype(jnp.bfloat16)  77.2 us
    psum x1, blocking collectives, shards(): rot_acts = lax.psum(partial_acts, NARROW).astype(jnp.bfloat16)  56.4 us
    psum x4, blocking collectives, over_axes(): return functools.reduce(lax.psum, axes, value)  36.2 us
    all_to_all x1, blocking collectives, shards(): lax.all_to_all(out_grads, WIDE, split_axis=1, concat_axis=0, tiled=True)  26.1 us
    dot_general x1, matrix products, shards(): jnp.dot(lax.all_gather(activations, WIDE, axis=0, tiled=True), basis_in,...  13.1 us
    dot_general x1, matrix products, shards(): jnp.einsum('ti,qij->qtj', rot_grads, precond, preferred_element_type=jnp....  8.92 us
  transfers between devices with their start and end apart: 2, of which 1 were waited for; matrix products, arithmetic and copies ran while one was open for 1% of the time, Pallas kernels for 0%

profile of v1, /device:TPU:1, one launch (start us, length us, event | category | flops | bytes accessed | tf_op | source)
XLA Modules:
  0.0 390.0 jit_solution(5097873965967763818)
XLA Ops:
  7.4 0.0 copy-start
  7.4 0.0 all-reduce.4.cloned.1.call-start
  7.4 1.2 copy.17
  8.5 26.1 %all_to_all.19 = bf16[32,32,256]{2,0,1:T(8,128)(2,1)S(1)} all-to-all(bf16[32,32,256]{2,0,1:T(8,128)(2,1)S(1)} %bitcast.22), channel_id=1, replica_groups=mesh['wide_0'=4,'wide_1'=8,'narrow_0'=4,'narrow_1'=2] {'wide_0','wide_1'}, dimensions={1} | all-to-all | bytes 1048576 | tf_op jit(solution)/shard_map/all_to_all | solution.py:26
  34.7 0.0 copy-done
  34.7 2.8 fusion.9
  37.4 0.0 copy-start.1
  37.4 0.0 all-reduce.4.cloned.1.call-update
  37.5 0.0 all-gather.2.cloned.1.call-start
  37.5 0.5 all-gather.2.cloned.1.call-update
  38.0 0.9 copy-done.1
  38.9 2.1 convert_add_fusion
  41.1 146.6 %all-reduce.4.cloned.1.call-done = f32[1024,1024]{1,0:T(8,128)} async-done(((f32[1024,1024]{1,0:T(8,128)}), f32[1024,1024]{1,0:T(8,128)}) %all-reduce.4.cloned.1.call-update) | async-done | bytes 4194320 | tf_op jit(solution)/shard_map/psum | solution.py:28
  187.6 77.2 %all-reduce.6 = bf16[1024,1024]{1,0:T(8,128)(2,1)} all-reduce(f32[1024,1024]{1,0:T(8,128)} %all-reduce.4.cloned.1.call-done), channel_id=1, replica_groups=mesh['wide_0'=4,'wide_1'=8,'narrow_0'=4,'narrow_1'=2] {'wide_0'}, use_global_device_ids=true, to_apply=%region_1.0 | all-reduce | flops 1048576 | bytes 6291456 | tf_op jit(solution)/shard_map/psum | solution.py:28
  264.8 13.1 %fusion.10 = f32[1024,896]{1,0:T(8,128)} fusion(bf16[1024,3584]{1,0:T(8,128)(2,1)} %all-gather.2.cloned.1.call-done, bf16[3584,896]{1,0:T(8,128)(2,1)} %param.9), kind=kOutput, calls=%fused_computation.14 | convolution fusion | flops 6576668672 | bytes 17432576 | tf_op jit(solution)/shard_map/dot_general | solution.py:20
  277.9 56.4 %all-reduce.5 = bf16[1024,896]{1,0:T(8,128)(2,1)S(1)} all-reduce(f32[1024,896]{1,0:T(8,128)} %fusion.10), channel_id=1, replica_groups=mesh['wide_0'=4,'wide_1'=8,'narrow_0'=4,'narrow_1'=2] {'narrow_0','narro..., use_global_device_ids=true, to_apply=%region_2.0 | all-reduce | flops 917504 | bytes 5505024 | tf_op jit(solution)/shard_map/psum | solution.py:25
  334.4 2.9 copy.13
  337.3 8.9 %fusion = f32[2,1024]{1,0:T(2,128)S(1)} fusion(f32[1024,896]{0,1:T(8,128)} %copy.13, bf16[1024,1024]{1,0:T(8,128)(2,1)} %all-reduce.6, bf16[2,1024,896]{2,1,0:T(8,128)(2,1)} %param.12, f32[1024,896]{1,0:T(8,128)} %convert_add_fusion), kind=kOutput, calls=%fused_computation.1 | convolution fusion | flops 3767269376 | bytes 13115392 | tf_op jit(solution)/shard_map/ti,qij->qtj/dot_general | solution.py:32
  346.2 0.0 copy-done.2
  346.2 0.2 fusion.7
  346.4 6.5 %psum.52 = f32[64,2]{0,1:T(2,128)S(1)} all-reduce(f32[64,2]{0,1:T(2,128)S(1)} %fusion.7), channel_id=1, replica_groups=mesh['wide_0'=4,'wide_1'=8,'narrow_0'=4,'narrow_1'=2] {'wide_0'}, use_global_device_ids=true, to_apply=%region_4.0 | all-reduce | flops 128 | bytes 1024 | tf_op jit(solution)/shard_map/psum | solution.py:16
  352.9 11.7 %psum.53 = f32[64,2]{0,1:T(2,128)S(1)} all-reduce(f32[64,2]{0,1:T(2,128)S(1)} %psum.52), channel_id=1, replica_groups=mesh['wide_0'=4,'wide_1'=8,'narrow_0'=4,'narrow_1'=2] {'wide_1'}, use_global_device_ids=true, to_apply=%region_5.0 | all-reduce | flops 128 | bytes 1024 | tf_op jit(solution)/shard_map/psum | solution.py:16
  364.6 9.8 %psum.54 = f32[64,2]{0,1:T(2,128)S(1)} all-reduce(f32[64,2]{0,1:T(2,128)S(1)} %psum.53), channel_id=1, replica_groups=mesh['wide_0'=4,'wide_1'=8,'narrow_0'=4,'narrow_1'=2] {'narrow_0'}, use_global_device_ids=true, to_apply=%region_6.0 | all-reduce | flops 128 | bytes 1024 | tf_op jit(solution)/shard_map/psum | solution.py:16
  374.4 8.1 %psum.55 = f32[64,2]{0,1:T(2,128)} all-reduce(f32[64,2]{0,1:T(2,128)S(1)} %psum.54), channel_id=1, replica_groups=mesh['wide_0'=4,'wide_1'=8,'narrow_0'=4,'narrow_1'=2] {'narrow_1'}, use_global_device_ids=true, to_apply=%region_7.0 | all-reduce | flops 128 | bytes 1024 | tf_op jit(solution)/shard_map/psum | solution.py:16
  (2 shorter events, 0.0 us)
Async XLA Ops:
  7.4 27.3 %copy-start = (bf16[256,1024]{1,0:T(8,128)(2,1)S(1)}, bf16[256,1024]{1,0:T(8,128)(2,1)}, u32[]{:S(2)}) copy-start(bf16[256,1024]{1,0:T(8,128)(2,1)} %param.10) | copy-start | bytes 1572868
  7.4 180.3 %all-reduce.4.cloned.1.call-start = ((), (), s32[]{:S(2)}) async-start(), calls=%async_computation.1 | async-start | bytes 8388608 | tf_op jit(solution)/shard_map/psum | solution.py:28
  37.4 1.5 copy-start.1
  37.5 227.4 %all-gather.2.cloned.1.call-start = ((), (), s32[]{:S(2)}) async-start(), calls=%async_computation.2 | async-start | bytes 7569408 | tf_op jit(solution)/shard_map/all_gather | solution.py:21
  337.3 8.9 %copy-start.2 = (s32[1024]{0:T(1024)S(1)}, s32[1024]{0:T(1024)}, u32[]{:S(2)}) copy-start(s32[1024]{0:T(1024)} %param.13) | copy-start | bytes 12292
Sparse Core Ops, SparseCore 0:
  37.6 150.0 all-reduce.3
Sparse Core Ops, SparseCore 1:
  40.5 144.5 all-gather.1
